TPU v7x, 32 devices: a whole 2x2x4 slice. The times are simulated.
32 devices in a mesh: fsdp: 8 (over z, core), seq: 4 (over y, x).
Axes of the slice: x: 2, y: 2, z: 4, core: 2. Of those that a mesh axis runs over, the one named last changes fastest.
Arguments:
- hidden_in: bfloat16 [8192, 1536], P(('fsdp', 'seq')), may hold values from -12 to 12
- cotangent: bfloat16 [8192, 1536], P(('fsdp', 'seq')), may hold values from -6 to 6
- segment_ids: int32 [8, 1024], P('fsdp', 'seq'), may hold values from 0 to 3, never falling along the last dimension, each value on 1 to 512 neighbouring positions
- w_qkv: bfloat16 [1536, 3072], P('fsdp', 'seq'), may hold values from -1.5 to 1.5
- w_out: bfloat16 [1536, 1536], P('fsdp', 'seq'), may hold values from -0.625 to 0.625
- w_gate: bfloat16 [1536, 4096], P('fsdp', 'seq'), may hold values from -0.15625 to 0.15625
- w_up: bfloat16 [1536, 4096], P('fsdp', 'seq'), may hold values from -0.15625 to 0.15625
- w_down: bfloat16 [4096, 1536], P('fsdp', 'seq'), may hold values from -0.09375 to 0.09375
- gain_attn: bfloat16 [1536], P(('fsdp', 'seq')), may hold values from 0.099609375 to 1.8984375
- gain_mlp: bfloat16 [1536], P(('fsdp', 'seq')), may hold values from 0.099609375 to 1.8984375
Outputs:
- output: float32 [8192, 1536], P(('fsdp', 'seq'))
- d_input: float32 [8192, 1536], P(('fsdp', 'seq'))
- g_qkv: float32 [1536, 3072], P('fsdp', 'seq')
- g_out: float32 [1536, 1536], P('fsdp', 'seq')
- g_gate: float32 [1536, 4096], P('fsdp', 'seq')
- g_up: float32 [1536, 4096], P('fsdp', 'seq')
- g_down: float32 [4096, 1536], P('fsdp', 'seq')
- g_gain_attn: float32 [1536], P(('fsdp', 'seq'))
- g_gain_mlp: float32 [1536], P(('fsdp', 'seq'))
Inputs may be any that keep to these rules, and one draw needn't show every extreme that they name: `segment_ids`: document numbers never fall along a row; a document has 1 to 512 tokens.
All inputs are finite; a program needn't handle non-finite values.
Results may differ from a plain program's by a relative error of at most 0.02.
Values may be sent and summed in bfloat16 or wider, within the bound.
A program may use at most 320 MiB of HBM per device.

v0:
```python
import math
import jax
import jax.numpy as jnp
from jax import lax
from jax.sharding import PartitionSpec as P

HEAD_DIM = 96
EPSILON = 1e-05
ROPE_BASE = 100000.0
NEGATIVE = -1e30


def rope_tables(ids):
    length = ids.shape[0]
    first = jnp.sum((ids[None, :] < ids[:, None]).astype(jnp.int32), axis=1)
    positions = jnp.arange(length, dtype=jnp.int32) - first
    half_dim = HEAD_DIM // 2
    freq_steps = jnp.arange(half_dim, dtype=jnp.float32)
    inverse = jnp.exp(freq_steps * (-2.0 * math.log(ROPE_BASE) / HEAD_DIM))
    angles = positions.astype(jnp.float32)[:, None] * inverse[None, :]
    return (jnp.cos(angles), jnp.sin(angles))


def rotate(block, cosine_table, sine_table):
    half_dim = block.shape[-1] // 2
    lower, upper = (block[..., :half_dim], block[..., half_dim:])
    return jnp.concatenate(
        [lower * cosine_table - upper * sine_table, upper * cosine_table + lower * sine_table],
        axis=-1,
    )


def inv_rms(values):
    return lax.rsqrt(jnp.mean(values * values, axis=-1, keepdims=True) + EPSILON)


def norm_back(grad_in, values, row_scale, gain_vec):
    weighted = grad_in * gain_vec
    d_values = row_scale * (
        weighted
        - values * (row_scale * row_scale) * jnp.mean(weighted * values, axis=-1, keepdims=True)
    )
    return (d_values, jnp.sum(grad_in * values * row_scale, axis=0))


def contract_rows(left, right):
    return lax.dot_general(
        left, right, (((0,), (0,)), ((), ())), preferred_element_type=jnp.float32
    )


def times(left, right):
    return jnp.dot(left, right, preferred_element_type=jnp.float32)


def times_trans(left, right):
    return lax.dot_general(
        left, right, (((1,), (1,)), ((), ())), preferred_element_type=jnp.float32
    )


def attend_forward(group, allowed, score_scale):
    queries, keys, vals = (group[:, :2], group[:, 2], group[:, 3])
    scores = jnp.einsum("qhd,kd->hqk", queries, keys, preferred_element_type=jnp.float32)
    scores = jnp.where(allowed[None], scores * score_scale, NEGATIVE)
    row_max = jnp.max(scores, axis=-1, keepdims=True)
    lse = row_max + jnp.log(jnp.sum(jnp.exp(scores - row_max), axis=-1, keepdims=True))
    weights = jnp.where(allowed[None], jnp.exp(scores - lse), 0.0).astype(jnp.bfloat16)
    mixed = jnp.einsum("hqk,kd->qhd", weights, vals, preferred_element_type=jnp.float32)
    return (mixed.astype(jnp.bfloat16), lse)


def attend_backward(group, mixed, lse, d_mixed, allowed, score_scale):
    queries, keys, vals = (group[:, :2], group[:, 2], group[:, 3])
    delta = jnp.sum(d_mixed.astype(jnp.float32) * mixed.astype(jnp.float32), axis=-1)
    scores = jnp.einsum("qhd,kd->hqk", queries, keys, preferred_element_type=jnp.float32)
    probs = jnp.where(allowed[None], jnp.exp(scores * score_scale - lse), 0.0)
    d_vals = jnp.einsum(
        "hqk,qhd->kd", probs.astype(jnp.bfloat16), d_mixed, preferred_element_type=jnp.float32
    )
    d_probs = jnp.einsum("qhd,kd->hqk", d_mixed, vals, preferred_element_type=jnp.float32)
    d_scores = (probs * (d_probs - jnp.transpose(delta)[:, :, None])).astype(jnp.bfloat16)
    d_q = jnp.einsum("hqk,kd->qhd", d_scores, keys, preferred_element_type=jnp.float32)
    d_k = jnp.einsum("hqk,qhd->kd", d_scores, queries, preferred_element_type=jnp.float32)
    return (d_q * score_scale, d_k * score_scale, d_vals)


def body(
    hidden_in, cotangent, segment_ids, w_qkv, w_out, w_gate, w_up, w_down, gain_attn, gain_mlp
):
    rows = hidden_in.shape[0]
    fsdp = lax.axis_size("fsdp")
    seq = lax.axis_size("seq")
    ratio = fsdp // seq
    scale = 1.0 / math.sqrt(HEAD_DIM)
    length = rows * seq
    moves = [
        (f * seq + s, (f % ratio * seq + s) * seq + f // ratio)
        for f in range(fsdp)
        for s in range(seq)
    ]
    back = [(there, here) for here, there in moves]

    def gather_rows(shard):
        height, width = shard.shape
        moved = lax.ppermute(shard, ("fsdp", "seq"), moves)
        blocks = lax.all_gather(moved, "fsdp", axis=0, tiled=False)
        blocks = blocks.reshape(ratio, seq, height, width)
        return jnp.transpose(blocks, (0, 2, 1, 3)).reshape(ratio * height, seq * width)

    def scatter_rows(grad):
        height, width = (grad.shape[0] // ratio, grad.shape[1] // seq)
        blocks = grad.astype(jnp.bfloat16).reshape(ratio, height, seq, width)
        blocks = jnp.transpose(blocks, (0, 2, 1, 3)).reshape(fsdp, height, width)
        own = lax.psum_scatter(blocks, "fsdp", scatter_dimension=0, tiled=False)
        return lax.ppermute(own, ("fsdp", "seq"), back).astype(jnp.float32)

    def gather_cols(shard):
        return lax.all_gather(shard, "fsdp", axis=0, tiled=True)

    def scatter_cols(grad):
        return lax.psum_scatter(
            grad.astype(jnp.bfloat16), "fsdp", scatter_dimension=0, tiled=True
        ).astype(jnp.float32)

    def gather_tokens(block):
        return lax.all_gather(block, "seq", axis=0, tiled=True)

    def scatter_tokens(partial):
        return lax.psum_scatter(
            partial.astype(jnp.bfloat16), "seq", scatter_dimension=0, tiled=True
        ).astype(jnp.float32)

    gains = lax.all_gather(
        jnp.stack([gain_attn, gain_mlp]), ("fsdp", "seq"), axis=1, tiled=True
    ).astype(jnp.float32)
    gain_one, gain_two = (gains[0], gains[1])
    ids = lax.all_gather(segment_ids, "seq", axis=1, tiled=True)[0]
    hidden_all = gather_tokens(hidden_in)
    cot_all = gather_tokens(cotangent)
    cols_qkv = gather_cols(w_qkv)
    rows_out = gather_rows(w_out)
    cols_gate = gather_cols(w_gate)
    cols_up = gather_cols(w_up)
    rows_down = gather_rows(w_down)
    tok = jnp.arange(length, dtype=jnp.int32)
    allowed = (ids[:, None] == ids[None, :]) & (tok[None, :] <= tok[:, None])
    cosine, sine = rope_tables(ids)
    values_all = hidden_all.astype(jnp.float32)
    normed_one = (values_all * inv_rms(values_all) * gain_one).astype(jnp.bfloat16)
    groups = cols_qkv.shape[1] // (4 * HEAD_DIM)
    projected = times(normed_one, cols_qkv).reshape(length, groups, 4, HEAD_DIM)
    packed = jnp.concatenate(
        [
            rotate(projected[:, :, :3], cosine[:, None, None, :], sine[:, None, None, :]),
            projected[:, :, 3:],
        ],
        axis=2,
    ).astype(jnp.bfloat16)
    forward = [attend_forward(packed[:, g], allowed, scale) for g in range(groups)]
    attn = jnp.stack([mixed for mixed, _ in forward], axis=1).reshape(length, -1)
    values_in = hidden_in.astype(jnp.float32)
    middle = values_in + scatter_tokens(times(attn, rows_out))
    scale_two = inv_rms(middle)
    normed_two = gather_tokens((middle * scale_two * gain_two).astype(jnp.bfloat16))
    gate = times(normed_two, cols_gate)
    up = times(normed_two, cols_up)
    sig = jax.nn.sigmoid(gate)
    activated = gate * sig
    hid = (activated * up).astype(jnp.bfloat16)
    output = middle + scatter_tokens(times(hid, rows_down))
    g_down = scatter_rows(contract_rows(hid, cot_all))
    d_hid = times_trans(cot_all, rows_down)
    d_gate = (d_hid * up * sig * (1.0 + gate * (1.0 - sig))).astype(jnp.bfloat16)
    d_up = (d_hid * activated).astype(jnp.bfloat16)
    g_gate = scatter_cols(contract_rows(normed_two, d_gate))
    g_up = scatter_cols(contract_rows(normed_two, d_up))
    d_normed_two = scatter_tokens(times_trans(d_gate, cols_gate) + times_trans(d_up, cols_up))
    d_middle, part_two = norm_back(d_normed_two, middle, scale_two, gain_two)
    d_middle = cotangent.astype(jnp.float32) + d_middle
    d_low = gather_tokens(d_middle.astype(jnp.bfloat16))
    g_out = scatter_rows(contract_rows(attn, d_low))
    d_attn = times_trans(d_low, rows_out).astype(jnp.bfloat16)
    d_attn = d_attn.reshape(length, groups, 2, HEAD_DIM)
    pieces = []
    for g in range(groups):
        d_q, d_k, d_v = attend_backward(
            packed[:, g], forward[g][0], forward[g][1], d_attn[:, g], allowed, scale
        )
        turned = rotate(
            jnp.concatenate([d_q, d_k[:, None]], axis=1), cosine[:, None, :], -sine[:, None, :]
        )
        pieces.append(jnp.concatenate([turned, d_v[:, None]], axis=1))
    d_packed = jnp.stack(pieces, axis=1).reshape(length, -1).astype(jnp.bfloat16)
    g_qkv = scatter_cols(contract_rows(normed_one, d_packed))
    d_normed_one = scatter_tokens(times_trans(d_packed, cols_qkv))
    d_tokens, part_one = norm_back(d_normed_one, values_in, inv_rms(values_in), gain_one)
    d_tokens = d_middle + d_tokens
    g_gains = lax.psum_scatter(
        jnp.stack([part_one, part_two]), ("fsdp", "seq"), scatter_dimension=1, tiled=True
    )
    return (output, d_tokens, g_qkv, g_out, g_gate, g_up, g_down, g_gains[0], g_gains[1])


def solution(mesh):
    both = P(("fsdp", "seq"), None)
    split = P("fsdp", "seq")
    gain = P(("fsdp", "seq"))
    in_specs = (both, both, split, split, split, split, split, split, gain, gain)
    out_specs = (both, both, split, split, split, split, split, gain, gain)
    return jax.shard_map(body, mesh=mesh, in_specs=in_specs, out_specs=out_specs, check_vma=False)
```

profile of v0, /device:TPU:0, one launch (start us, length us, event | category | flops | bytes accessed | tf_op | source)
XLA Modules:
  0.0 949.5 jit_solution(4358844575518664176)
XLA Ops:
  11.7 74.6 %all-gather.2 = bf16[32,48,2]{1,2,0:T(2,128)(2,1)S(1)} all-gather(bf16[1,48,2]{1,2,0:T(2,128)(2,1)S(1)} %maximum_bitcast_fusion.2), channel_id=1, replica_groups=mesh['fsdp'=8,'seq'=4] {'fsdp','seq'}, dimensions={0}, use_global_device_ids=true | all-gather | bytes 6336 | tf_op jit(solution)/shard_map/all_gather | solution.py:134
  86.4 7.2 all_gather.42
  96.3 2.6 copy.58
  100.0 2.6 fusion.12
  102.6 20.0 %all-gather.15.cloned.1.call-done = bf16[1536,768]{1,0:T(8,128)(2,1)} async-done(((bf16[192,768]{1,0:T(8,128)(2,1)}), bf16[1536,768]{1,0:T(8,128)(2,1)}) %all-gather.15.cloned.1.call-update) | async-done | bytes 2359312 | tf_op jit(solution)/shard_map/all_gather | solution.py:119
  122.6 5.5 fusion.69
  130.8 4.1 exponential_reduce_fusion.1
  138.3 2.9 fusion.44
  141.3 2.9 fusion.45
  145.2 3.5 convolution_convert_fusion.1
  151.8 47.1 %reduce-scatter.13.cloned.1.call-done = bf16[256,1536]{1,0:T(8,128)(2,1)} async-done(((bf16[1024,1536]{1,0:T(8,128)(2,1)}), bf16[256,1536]{1,0:T(8,128)(2,1)}) %reduce-scatter.13.cloned.1.call-update) | async-done | bytes 786448 | tf_op jit(solution)/shard_map/reduce_scatter | solution.py:130
  204.4 34.8 %all-gather.29.cloned.1.call-done = bf16[4096,384]{1,0:T(8,128)(2,1)} async-done(((bf16[512,384]{1,0:T(8,128)(2,1)}), bf16[4096,384]{1,0:T(8,128)(2,1)}) %all-gather.29.cloned.1.call-update) | async-done | bytes 3145744 | tf_op jit(solution)/shard_map/all_gather | solution.py:107
  239.2 4.3 copy.59
  245.8 32.1 %all-gather.21.cloned.1.call-done = bf16[1536,1024]{1,0:T(8,128)(2,1)} async-done(((bf16[192,1024]{1,0:T(8,128)(2,1)}), bf16[1536,1024]{1,0:T(8,128)(2,1)}) %all-gather.21.cloned.1.call-update) | async-done | bytes 3145744 | tf_op jit(solution)/shard_map/all_gather | solution.py:119
  277.9 45.3 %all-gather.17.cloned.1.call-done = bf16[1024,1536]{1,0:T(8,128)(2,1)} async-done(((bf16[256,1536]{1,0:T(8,128)(2,1)}), bf16[1024,1536]{1,0:T(8,128)(2,1)}) %all-gather.17.cloned.1.call-update) | async-done | bytes 3145744 | tf_op jit(solution)/shard_map/all_gather | solution.py:127
  323.2 8.3 fusion.95
  331.4 31.7 %all-gather.19.cloned.1.call-done = bf16[1536,1024]{1,0:T(8,128)(2,1)} async-done(((bf16[192,1024]{1,0:T(8,128)(2,1)}), bf16[1536,1024]{1,0:T(8,128)(2,1)}) %all-gather.19.cloned.1.call-update) | async-done | bytes 3145744 | tf_op jit(solution)/shard_map/all_gather | solution.py:119
  363.1 8.2 fusion.94
  371.4 36.5 %all-gather.23.cloned.1.call-done = bf16[1024,1536]{1,0:T(8,128)(2,1)} async-done(((bf16[256,1536]{1,0:T(8,128)(2,1)}), bf16[1024,1536]{1,0:T(8,128)(2,1)}) %all-gather.23.cloned.1.call-update) | async-done | bytes 3145744 | tf_op jit(solution)/shard_map/all_gather | solution.py:127
  407.8 11.6 %multiply_convert_fusion = (bf16[1024,1024]{1,0:T(8,128)(2,1)S(1)}, bf16[1024,1024]{1,0:T(8,128)(2,1)S(1)}, bf16[1024,1024]{1,0:T(8,128)(2,1)}) fusion(f32[1024,1024]{1,0:T(8,128)} %fusion.94, f32[1024,1024]{1,0:T(8,128)} %fusion.95, bf16[1024,1536]{1,0:T(8,128)(2,1)} %all-gather.23.cloned.1.call-done, bf16[1024,1536]{1,0:T(8,128)(2,1)} %bitcast.230), kind=kOutput, calls=%fused_computation.28 | convolution fusion | flops 3236954112 | bytes 20971520 | tf_op jit(solution)/shard_map/dot_general | solution.py:57
  419.4 3.9 fusion.96
  423.4 5.0 add_convert_fusion
  428.4 44.0 %reduce-scatter.17.cloned.1.call-done = bf16[256,1536]{1,0:T(8,128)(2,1)} async-done(((bf16[1024,1536]{1,0:T(8,128)(2,1)}), bf16[256,1536]{1,0:T(8,128)(2,1)}) %reduce-scatter.17.cloned.1.call-update) | async-done | bytes 786448 | tf_op jit(solution)/shard_map/reduce_scatter | solution.py:130
  474.9 2.7 fusion.92
  477.7 7.6 convolution_convert_fusion.2
  485.3 6.3 reshape.273
  491.6 3.9 copy.67
  495.6 7.7 convolution_convert_fusion.3
  503.4 7.7 convolution_convert_fusion.4
  511.3 10.4 %all-gather.25.cloned.1.call-done = bf16[1024,1536]{1,0:T(8,128)(2,1)} async-done(((bf16[256,1536]{1,0:T(8,128)(2,1)}), bf16[1024,1536]{1,0:T(8,128)(2,1)}) %all-gather.25.cloned.1.call-update) | async-done | bytes 3145744 | tf_op jit(solution)/shard_map/all_gather | solution.py:127
  521.8 4.3 convolution_convert_fusion.7
  526.1 2.5 reshape.271
  529.8 3.8 convolution_convert_fusion.8
  534.0 5.4 fusion.3
  541.6 3.1 fusion.1
  551.8 5.7 fusion.62
  557.7 5.7 fusion.65
  565.3 4.4 convolution_convert_fusion.6
  569.8 5.8 convolution_convert_fusion
  575.6 7.7 convolution_convert_fusion.5
  585.7 42.7 %reduce-scatter.27.cloned.1.call-done = bf16[192,1024]{1,0:T(8,128)(2,1)} async-done(((bf16[1536,1024]{1,0:T(8,128)(2,1)}), bf16[192,1024]{1,0:T(8,128)(2,1)}) %reduce-scatter.27.cloned.1.call-update) | async-done | bytes 393232 | tf_op jit(solution)/shard_map/reduce_scatter | solution.py:122
  630.3 42.6 %reduce-scatter.25.cloned.1.call-done = bf16[192,1024]{1,0:T(8,128)(2,1)} async-done(((bf16[1536,1024]{1,0:T(8,128)(2,1)}), bf16[192,1024]{1,0:T(8,128)(2,1)}) %reduce-scatter.25.cloned.1.call-update) | async-done | bytes 393232 | tf_op jit(solution)/shard_map/reduce_scatter | solution.py:122
  674.9 32.4 %reduce-scatter.23.cloned.1.call-done = bf16[1,192,384]{2,1,0:T(8,128)(2,1)} async-done(((bf16[8,192,384]{2,1,0:T(8,128)(2,1)}), bf16[1,192,384]{2,1,0:T(8,128)(2,1)}) %reduce-scatter.23.cloned.1.call-update) | async-done | bytes 147472 | tf_op jit(solution)/shard_map/reduce_scatter | solution.py:115
  711.8 32.7 %reduce-scatter.21.cloned.1.call-done = bf16[192,768]{1,0:T(8,128)(2,1)} async-done(((bf16[1536,768]{1,0:T(8,128)(2,1)}), bf16[192,768]{1,0:T(8,128)(2,1)}) %reduce-scatter.21.cloned.1.call-update) | async-done | bytes 294928 | tf_op jit(solution)/shard_map/reduce_scatter | solution.py:122
  746.4 46.8 %reduce-scatter.19.cloned.1.call-done = bf16[256,1536]{1,0:T(8,128)(2,1)} async-done(((bf16[1024,1536]{1,0:T(8,128)(2,1)}), bf16[256,1536]{1,0:T(8,128)(2,1)}) %reduce-scatter.19.cloned.1.call-update) | async-done | bytes 786448 | tf_op jit(solution)/shard_map/reduce_scatter | solution.py:130
  796.8 43.3 %reduce-scatter.15.cloned.1.call-done = bf16[256,1536]{1,0:T(8,128)(2,1)} async-done(((bf16[1024,1536]{1,0:T(8,128)(2,1)}), bf16[256,1536]{1,0:T(8,128)(2,1)}) %reduce-scatter.15.cloned.1.call-update) | async-done | bytes 786448 | tf_op jit(solution)/shard_map/reduce_scatter | solution.py:130
  840.1 4.1 fusion.31
  844.2 96.5 %reduce-scatter.31.cloned.1.call-done = f32[48,2]{1,0:T(8,128)} async-done(((f32[1536,2]{1,0:T(8,128)}), f32[48,2]{1,0:T(8,128)}) %reduce-scatter.31.cloned.1.call-update) | async-done | bytes 400
  (204 shorter events, 59.8 us)
Async XLA Ops:
  7.2 89.1 %all-gather.27.cloned.1.call-start = ((), (), s32[]{:S(2)}) async-start(), calls=%async_computation.26 | async-start | bytes 1327104 | tf_op jit(solution)/shard_map/all_gather | solution.py:107
  7.2 1.6 collective-permute-start
  9.5 90.5 %all-gather.13.cloned.1.call-start = ((), (), s32[]{:S(2)}) async-start(), calls=%async_computation.10 | async-start | bytes 3932160 | tf_op jit(solution)/shard_map/all_gather | solution.py:127
  10.2 112.4 %all-gather.15.cloned.1.call-start = ((), (), s32[]{:S(2)}) async-start(), calls=%async_computation.11 | async-start | bytes 2654208 | tf_op jit(solution)/shard_map/all_gather | solution.py:119
  11.0 187.9 %reduce-scatter.13.cloned.1.call-start = ((), (), s32[]{:S(2)}) async-start(), calls=%async_computation.12 | async-start | bytes 3932160 | tf_op jit(solution)/shard_map/reduce_scatter | solution.py:130
  95.6 32.6 %copy-start.13 = (f32[1024,48]{0,1:T(8,128)}, f32[1024,48]{0,1:T(8,128)S(1)}, u32[]{:S(2)}) copy-start(f32[1024,48]{0,1:T(8,128)S(1)} %get-tuple-element.39) | copy-start | bytes 589828
  96.2 45.0 %copy-start.6 = (pred[1024,1024]{0,1:T(8,128)(4,1)}, pred[1024,1024]{0,1:T(8,128)(4,1)S(1)}, u32[]{:S(2)}) copy-start(pred[1024,1024]{0,1:T(8,128)(4,1)S(1)} %fusion.22) | copy-start | bytes 3145732
  102.6 25.6 %copy-start.42 = (f32[1024]{0:T(1024)}, f32[1024]{0:T(1024)S(1)}, u32[]{:S(2)}) copy-start(f32[1024]{0:T(1024)S(1)} %add_rsqrt_fusion) | copy-start | bytes 12292
  128.9 12.3 %copy-start.11 = (bf16[1024,4,96]{0,2,1:T(8,128)(2,1)}, bf16[1024,4,96]{0,2,1:T(8,128)(2,1)S(1)}, u32[]{:S(2)}) copy-start(bf16[1024,4,96]{0,2,1:T(8,128)(2,1)S(1)} %get-tuple-element.31) | copy-start | bytes 2359300
  128.9 415.8 %copy-start.10 = (bf16[1024,4,96]{0,2,1:T(8,128)(2,1)}, bf16[1024,4,96]{0,2,1:T(8,128)(2,1)S(1)}, u32[]{:S(2)}) copy-start(bf16[1024,4,96]{0,2,1:T(8,128)(2,1)S(1)} %get-tuple-element.32) | copy-start | bytes 2359300
  130.8 10.4 %copy-start.47 = (f32[1024,1024,2]{1,0,2:T(8,128)}, f32[1024,1024,2]{1,0,2:T(8,128)S(1)}, u32[]{:S(2)}) copy-start(f32[1024,1024,2]{1,0,2:T(8,128)S(1)} %get-tuple-element.45) | copy-start | bytes 25165828
  148.7 50.1 %copy-start = (bf16[256,1536]{1,0:T(8,128)(2,1)S(1)}, bf16[256,1536]{1,0:T(8,128)(2,1)}, u32[]{:S(2)}) copy-start(bf16[256,1536]{1,0:T(8,128)(2,1)} %param.10) | copy-start | bytes 2359300
  148.7 90.5 %all-gather.29.cloned.1.call-start = ((), (), s32[]{:S(2)}) async-start(), calls=%async_computation.27 | async-start | bytes 3538944 | tf_op jit(solution)/shard_map/all_gather | solution.py:107
  149.7 0.7 collective-permute-start.1
  151.2 126.7 %all-gather.21.cloned.1.call-start = ((), (), s32[]{:S(2)}) async-start(), calls=%async_computation.15 | async-start | bytes 3538944 | tf_op jit(solution)/shard_map/all_gather | solution.py:119
  151.7 171.4 %all-gather.17.cloned.1.call-start = ((), (), s32[]{:S(2)}) async-start(), calls=%async_computation.13 | async-start | bytes 3932160 | tf_op jit(solution)/shard_map/all_gather | solution.py:127
  200.3 274.6 %copy-start.28 = (f32[256]{0:T(256)}, f32[256]{0:T(256)S(1)}, u32[]{:S(2)}) copy-start(f32[256]{0:T(256)S(1)} %get-tuple-element.43) | copy-start | bytes 3076
  200.3 274.6 %copy-start.31 = (f32[256]{0:T(256)}, f32[256]{0:T(256)S(1)}, u32[]{:S(2)}) copy-start(f32[256]{0:T(256)S(1)} %get-tuple-element.42) | copy-start | bytes 3076
  202.7 160.5 %all-gather.19.cloned.1.call-start = ((), (), s32[]{:S(2)}) async-start(), calls=%async_computation.14 | async-start | bytes 3538944 | tf_op jit(solution)/shard_map/all_gather | solution.py:119
  203.4 204.4 %all-gather.23.cloned.1.call-start = ((), (), s32[]{:S(2)}) async-start(), calls=%async_computation.17 | async-start | bytes 3932160 | tf_op jit(solution)/shard_map/all_gather | solution.py:127
  204.2 268.3 %reduce-scatter.17.cloned.1.call-start = ((), (), s32[]{:S(2)}) async-start(), calls=%async_computation.18 | async-start | bytes 3932160 | tf_op jit(solution)/shard_map/reduce_scatter | solution.py:130
  407.8 11.6 %copy-start.45 = (bf16[1536,1024]{1,0:T(8,128)(2,1)S(1)}, bf16[1536,1024]{1,0:T(8,128)(2,1)}, u32[]{:S(2)}) copy-start(bf16[1536,1024]{1,0:T(8,128)(2,1)} %all-gather.19.cloned.1.call-done) | copy-start | bytes 9437188
  428.4 44.1 %copy-start.1 = (bf16[256,1536]{1,0:T(8,128)(2,1)S(1)}, bf16[256,1536]{1,0:T(8,128)(2,1)}, u32[]{:S(2)}) copy-start(bf16[256,1536]{1,0:T(8,128)(2,1)} %reduce-scatter.13.cloned.1.call-done) | copy-start | bytes 2359300
  428.4 46.6 %copy-start.3 = (bf16[256,1536]{1,0:T(8,128)(2,1)S(1)}, bf16[256,1536]{1,0:T(8,128)(2,1)}, u32[]{:S(2)}) copy-start(bf16[256,1536]{1,0:T(8,128)(2,1)} %param.11) | copy-start | bytes 2359300
  428.4 93.4 %all-gather.25.cloned.1.call-start = ((), (), s32[]{:S(2)}) async-start(), calls=%async_computation.19 | async-start | bytes 3932160 | tf_op jit(solution)/shard_map/all_gather | solution.py:127
  474.9 10.4 %copy-start.33 = (f32[256]{0:T(256)}, f32[256]{0:T(256)S(1)}, u32[]{:S(2)}) copy-start(f32[256]{0:T(256)S(1)} %broadcast_multiply_fusion.1) | copy-start | bytes 3076
  477.7 105.7 %reduce-scatter.29.cloned.1.call-start = ((), (), s32[]{:S(2)}) async-start(), calls=%async_computation.25 | async-start | bytes 3538944 | tf_op jit(solution)/shard_map/reduce_scatter | solution.py:115
  495.6 132.8 %reduce-scatter.27.cloned.1.call-start = ((), (), s32[]{:S(2)}) async-start(), calls=%async_computation.24 | async-start | bytes 3538944 | tf_op jit(solution)/shard_map/reduce_scatter | solution.py:122
  503.3 169.6 %reduce-scatter.25.cloned.1.call-start = ((), (), s32[]{:S(2)}) async-start(), calls=%async_computation.23 | async-start | bytes 3538944 | tf_op jit(solution)/shard_map/reduce_scatter | solution.py:122
  511.1 10.7 %copy-start.21 = (bf16[1024,2,2,96]{0,3,2,1:T(8,128)(2,1)S(1)}, bf16[1024,2,2,96]{0,3,2,1:T(8,128)(2,1)}, u32[]{:S(2)}) copy-start(bf16[1024,2,2,96]{0,3,2,1:T(8,128)(2,1)} %copy-done.20) | copy-start | bytes 2359300
  511.1 196.2 %reduce-scatter.23.cloned.1.call-start = ((), (), s32[]{:S(2)}) async-start(), calls=%async_computation.22 | async-start | bytes 1327104 | tf_op jit(solution)/shard_map/reduce_scatter | solution.py:115
  529.8 11.8 %slice-start = ((s8[8388608]{0:T(1024)(128)(4,1)}), s8[4194304]{0:T(1024)(128)(4,1)S(1)}, s32[]{:S(2)}) async-start(s8[8388608]{0:T(1024)(128)(4,1)} %bitcast.225), calls=%async_computation.29 | async-start | bytes 8388608
  533.6 7.9 copy-start.22
  534.0 7.6 slice-start.1
  549.6 195.0 %reduce-scatter.21.cloned.1.call-start = ((), (), s32[]{:S(2)}) async-start(), calls=%async_computation.21 | async-start | bytes 2654208 | tf_op jit(solution)/shard_map/reduce_scatter | solution.py:122
  551.8 5.8 copy-start.37
  569.8 223.5 %reduce-scatter.19.cloned.1.call-start = ((), (), s32[]{:S(2)}) async-start(), calls=%async_computation.20 | async-start | bytes 3932160 | tf_op jit(solution)/shard_map/reduce_scatter | solution.py:130
  575.6 264.5 %reduce-scatter.15.cloned.1.call-start = ((), (), s32[]{:S(2)}) async-start(), calls=%async_computation.16 | async-start | bytes 3932160 | tf_op jit(solution)/shard_map/reduce_scatter | solution.py:130
  583.3 357.4 %reduce-scatter.31.cloned.1.call-start = ((), (), s32[]{:S(2)}) async-start(), calls=%async_computation.28 | async-start | bytes 811008
  583.4 126.7 %collective-permute-start.3 = (bf16[512,384]{1,0:T(8,128)(2,1)}, bf16[512,384]{1,0:T(8,128)(2,1)S(1)}, u32[]{:S(2)}, u32[]{:S(2)}) collective-permute-start(bf16[512,384]{1,0:T(8,128)(2,1)} %bitcast.258), channel_id=1, source_target_pairs={{0,0},{4,1},{8,2},{12,3},{16,4},{20,5},{24,6},{28,7},{1,8},{5,9},{... | collective-permute-start | bytes 1179656 | tf_op jit(solution)/shard_map/ppermute | solution.py:116
  674.9 165.1 %copy-start.4 = (bf16[256,1536]{1,0:T(8,128)(2,1)S(1)}, bf16[256,1536]{1,0:T(8,128)(2,1)}, u32[]{:S(2)}) copy-start(bf16[256,1536]{1,0:T(8,128)(2,1)} %param.11) | copy-start | bytes 2359300
  674.9 165.1 %copy-start.5 = (bf16[256,1536]{1,0:T(8,128)(2,1)S(1)}, bf16[256,1536]{1,0:T(8,128)(2,1)}, u32[]{:S(2)}) copy-start(bf16[256,1536]{1,0:T(8,128)(2,1)} %reduce-scatter.17.cloned.1.call-done) | copy-start | bytes 2359300
  707.3 3.8 collective-permute-start.2
  711.1 129.0 %copy-start.29 = (f32[256]{0:T(256)S(1)}, f32[256]{0:T(256)}, u32[]{:S(2)}) copy-start(f32[256]{0:T(256)} %copy-done.28) | copy-start | bytes 3076
  711.1 129.0 %copy-start.30 = (f32[256]{0:T(256)S(1)}, f32[256]{0:T(256)}, u32[]{:S(2)}) copy-start(f32[256]{0:T(256)} %get-tuple-element.41) | copy-start | bytes 3076
  711.1 129.0 %copy-start.32 = (f32[256]{0:T(256)S(1)}, f32[256]{0:T(256)}, u32[]{:S(2)}) copy-start(f32[256]{0:T(256)} %copy-done.31) | copy-start | bytes 3076
  711.1 129.0 %copy-start.34 = (f32[256]{0:T(256)S(1)}, f32[256]{0:T(256)}, u32[]{:S(2)}) copy-start(f32[256]{0:T(256)} %copy-done.33) | copy-start | bytes 3076
  711.1 129.0 %copy-start.41 = (f32[256]{0:T(256)S(1)}, f32[256]{0:T(256)}, u32[]{:S(2)}) copy-start(f32[256]{0:T(256)} %get-tuple-element.40) | copy-start | bytes 3076
  (27 other events, 76.4 us)
Sparse Core Ops, SparseCore 0:
  10.2 33.3 all-gather.26
  45.4 43.8 all-gather.12
  91.0 31.6 all-gather.14
  148.8 49.9 reduce-scatter.12
  200.9 38.2 all-gather.28
  240.7 37.1 all-gather.20
  280.3 42.8 all-gather.16
  324.8 38.2 all-gather.18
  365.0 42.8 all-gather.22
  428.5 43.9 reduce-scatter.16
  477.8 43.9 all-gather.24
  523.9 40.3 reduce-scatter.28
  566.6 61.7 reduce-scatter.26
  630.5 42.3 reduce-scatter.24
  675.7 31.6 reduce-scatter.22
  709.5 35.0 reduce-scatter.20
  747.4 45.7 reduce-scatter.18
  796.1 43.9 reduce-scatter.14
  845.2 95.4 reduce-scatter.30
where the time goes:
time: 960 us; the launch traced here: 950 us
  waiting for transfers between devices  643 us (67%)
  matrix products  134 us (14%)
  blocking collectives  81.8 us (9%)
  other arithmetic  34.8 us (4%)
  local copies, waits for them, and re-layouts  34.7 us (4%)
  between operations  15 us (2%)
    reduce_scatter x4, waiting for transfers between devices, scatter_tokens(): lax.psum_scatter(partial.astype(jnp.bfloat16), 'seq', scatter_dimension=0...  181 us
    reduce_scatter x3, waiting for transfers between devices, scatter_cols(): lax.psum_scatter(grad.astype(jnp.bfloat16), 'fsdp', scatter_dimension=0,...  118 us
    unnamed x20, waiting for transfers between devices  100 us
    all_gather x4, waiting for transfers between devices, gather_tokens(): return lax.all_gather(block, 'seq', axis=0, tiled=True)  92.2 us
    all_gather x3, waiting for transfers between devices, gather_cols(): return lax.all_gather(shard, 'fsdp', axis=0, tiled=True)  83.8 us
    all_gather x1, blocking collectives, body(): lax.all_gather(jnp.stack([gain_attn, gain_mlp]), ('fsdp', 'seq'), axis=1,...  74.6 us
    all_gather x2, waiting for transfers between devices, gather_rows(): blocks = lax.all_gather(moved, 'fsdp', axis=0, tiled=False)  34.9 us
    dot_general x5, matrix products, times(): return jnp.dot(left, right, preferred_element_type=jnp.float32)  33.2 us
  transfers between devices with their start and end apart: 23, of which 16 were waited for; matrix products, arithmetic and copies ran while one was open for 15% of the time, Pallas kernels for 0%

commit v1 on v0

--- a/solution.py
+++ b/solution.py
@@ -8,6 +8,19 @@
 EPSILON = 1e-05
 ROPE_BASE = 100000.0
 NEGATIVE = -1e30
+
+
+def ring_gather(value, axis, dim):
+    ways = lax.axis_size(axis)
+    up = [(d, (d + 1) % ways) for d in range(ways)]
+    down = [(d, (d - 1) % ways) for d in range(ways)]
+    earlier, later = ([value], [value])
+    for _ in range(ways // 2):
+        earlier.append(lax.ppermute(earlier[-1], axis, up))
+    for _ in range((ways - 1) // 2):
+        later.append(lax.ppermute(later[-1], axis, down))
+    line = jnp.concatenate([*earlier[::-1], *later[1:]], axis=dim)
+    return jnp.roll(line, (lax.axis_index(axis) - ways // 2) * value.shape[dim], axis=dim)
 
 
 def rope_tables(ids):
@@ -116,7 +129,7 @@
         return lax.ppermute(own, ("fsdp", "seq"), back).astype(jnp.float32)
 
     def gather_cols(shard):
-        return lax.all_gather(shard, "fsdp", axis=0, tiled=True)
+        return ring_gather(shard, "fsdp", 0)
 
     def scatter_cols(grad):
         return lax.psum_scatter(

time: 960 us -> 922 us (0.960)
  waiting for transfers between devices: 643 us -> 553 us
  starting transfers between devices: 6.78 us -> 54.9 us
  local copies, waits for them, and re-layouts: 34.7 us -> 54.3 us
    all_gather x3 -> x0, waiting for transfers between devices: 83.8 us -> none  [gather_cols(): return lax.all_gather(shard, 'fsdp', axis=0, tiled=True)]
    ppermute x0 -> x21, waiting for transfers between devices: none -> 78 us  [the longest x12 72.1 us: ring_gather(): earlier.append(lax.ppermute(earlier[-1], axis, up))]
    ppermute x0 -> x21, starting transfers between devices: none -> 47.9 us  [the longest x9 34.9 us: ring_gather(): later.append(lax.ppermute(later[-1], axis, down))]
    all_gather x4, waiting for transfers between devices: 92.2 us -> 47.5 us  [gather_tokens(): return lax.all_gather(block, 'seq', axis=0, tiled=True)]
    all_gather x2, waiting for transfers between devices: 34.9 us -> 0.01 us  [gather_rows(): blocks = lax.all_gather(moved, 'fsdp', axis=0, tiled=False)]
    unnamed x109 -> x152, local copies, waits for them, and re-layouts: 12.2 us -> 30.6 us
    unnamed x20 -> x17, waiting for transfers between devices: 100 us -> 97.8 us
  transfers between devices with their start and end apart: 23 -> 41, of which waited for: 16 -> 24; matrix products, arithmetic and copies ran while one was open for 15% -> 17% of each run, Pallas kernels for 0% -> 0%
where the time goes in v1:
time: 922 us; the launch traced here: 917 us
  waiting for transfers between devices  553 us (60%)
  matrix products  132 us (14%)
  blocking collectives  72.3 us (8%)
  starting transfers between devices  54.9 us (6%)
  local copies, waits for them, and re-layouts  54.3 us (6%)
  other arithmetic  35.7 us (4%)
  between operations  15.2 us (2%)
    reduce_scatter x4, waiting for transfers between devices, scatter_tokens(): lax.psum_scatter(partial.astype(jnp.bfloat16), 'seq', scatter_dimension=0...  178 us
    reduce_scatter x3, waiting for transfers between devices, scatter_cols(): lax.psum_scatter(grad.astype(jnp.bfloat16), 'fsdp', scatter_dimension=0,...  118 us
    unnamed x17, waiting for transfers between devices  97.8 us
    ppermute x12, waiting for transfers between devices, ring_gather(): earlier.append(lax.ppermute(earlier[-1], axis, up))  72.1 us
    all_gather x1, blocking collectives, body(): lax.all_gather(jnp.stack([gain_attn, gain_mlp]), ('fsdp', 'seq'), axis=1,...  66.1 us
    all_gather x4, waiting for transfers between devices, gather_tokens(): return lax.all_gather(block, 'seq', axis=0, tiled=True)  47.5 us
    ppermute x9, starting transfers between devices, ring_gather(): later.append(lax.ppermute(later[-1], axis, down))  34.9 us
    reduce_scatter x2, waiting for transfers between devices, scatter_rows(): own = lax.psum_scatter(blocks, 'fsdp', scatter_dimension=0, tiled=False)  32.7 us
  transfers between devices with their start and end apart: 41, of which 24 were waited for; matrix products, arithmetic and copies ran while one was open for 17% of the time, Pallas kernels for 0%

profile of v1, /device:TPU:0, one launch (start us, length us, event | category | flops | bytes accessed | tf_op | source)
XLA Modules:
  0.0 917.5 jit_solution(246414644441899815)
XLA Ops:
  10.4 6.9 collective-permute-start
  17.4 7.4 collective-permute-start.4
  25.4 66.1 %all-gather.2 = bf16[32,48,2]{1,2,0:T(2,128)(2,1)S(1)} all-gather(bf16[1,48,2]{1,2,0:T(2,128)(2,1)S(1)} %maximum_bitcast_fusion.2), channel_id=1, replica_groups=mesh['fsdp'=8,'seq'=4] {'fsdp','seq'}, dimensions={0}, use_global_device_ids=true | all-gather | bytes 6336 | tf_op jit(solution)/shard_map/all_gather | solution.py:147
  91.6 6.3 all_gather.32
  98.5 8.0 collective-permute-done.1
  111.5 3.9 collective-permute-done.2
  116.1 4.1 collective-permute-start.6
  120.1 3.9 collective-permute-done.3
  142.1 4.7 fusion.30
  170.1 44.7 %reduce-scatter.13.cloned.1.call-done = bf16[256,1536]{1,0:T(8,128)(2,1)} async-done(((bf16[1024,1536]{1,0:T(8,128)(2,1)}), bf16[256,1536]{1,0:T(8,128)(2,1)}) %reduce-scatter.13.cloned.1.call-update) | async-done | bytes 786448 | tf_op jit(solution)/shard_map/reduce_scatter | solution.py:143
  220.9 7.5 collective-permute-done.15
  232.0 9.4 %collective-permute-done.8 = bf16[192,1024]{1,0:T(8,128)(2,1)S(1)} collective-permute-done((bf16[192,1024]{1,0:T(8,128)(2,1)S(1)}, bf16[192,1024]{1,0:T(8,128)(2,1)S(1)}, u32[]{:S(2)}, u32[]{:S(2)}) %collective-permute-start.8) | collective-permute-done | bytes 393248 | tf_op jit(solution)/shard_map/ppermute | solution.py:19
  241.4 16.8 %collective-permute-done.16 = bf16[192,1024]{1,0:T(8,128)(2,1)S(1)} collective-permute-done((bf16[192,1024]{1,0:T(8,128)(2,1)S(1)}, bf16[192,1024]{1,0:T(8,128)(2,1)S(1)}, u32[]{:S(2)}, u32[]{:S(2)}) %collective-permute-start.16) | collective-permute-done | bytes 393248 | tf_op jit(solution)/shard_map/ppermute | solution.py:19
  261.8 4.9 collective-permute-done.19
  266.7 5.7 collective-permute-start.20
  275.5 6.7 collective-permute-done.17
  292.5 6.5 collective-permute-done.18
  299.2 8.3 collective-permute-done.11
  315.5 4.3 copy.59
  322.1 8.3 fusion.107
  330.4 37.1 %all-gather.12.cloned.1.call-done = bf16[1024,1536]{1,0:T(8,128)(2,1)} async-done(((bf16[256,1536]{1,0:T(8,128)(2,1)}), bf16[1024,1536]{1,0:T(8,128)(2,1)}) %all-gather.12.cloned.1.call-update) | async-done | bytes 3145744 | tf_op jit(solution)/shard_map/all_gather | solution.py:140
  367.5 6.8 fusion.102
  374.3 8.3 multiply_convert_fusion.1
  382.6 4.4 fusion.104
  387.0 9.1 add_convert_fusion
  396.6 43.7 %reduce-scatter.17.cloned.1.call-done = bf16[256,1536]{1,0:T(8,128)(2,1)} async-done(((bf16[1024,1536]{1,0:T(8,128)(2,1)}), bf16[256,1536]{1,0:T(8,128)(2,1)}) %reduce-scatter.17.cloned.1.call-update) | async-done | bytes 786448 | tf_op jit(solution)/shard_map/reduce_scatter | solution.py:143
  445.5 7.7 convolution_convert_fusion.2
  453.2 6.2 reshape.273
  459.5 4.0 copy.67
  463.6 7.6 convolution_convert_fusion.4
  471.4 7.7 convolution_convert_fusion.3
  479.2 10.4 %all-gather.16.cloned.1.call-done = bf16[1024,1536]{1,0:T(8,128)(2,1)} async-done(((bf16[256,1536]{1,0:T(8,128)(2,1)}), bf16[1024,1536]{1,0:T(8,128)(2,1)}) %all-gather.16.cloned.1.call-update) | async-done | bytes 3145744 | tf_op jit(solution)/shard_map/all_gather | solution.py:140
  489.6 4.3 convolution_convert_fusion.7
  497.6 3.8 convolution_convert_fusion.8
  501.8 5.4 fusion.3
  519.7 5.7 fusion.67
  525.5 5.7 fusion.70
  533.2 4.4 convolution_convert_fusion.6
  537.7 5.8 convolution_convert_fusion
  543.5 7.6 convolution_convert_fusion.5
  553.5 42.7 %reduce-scatter.25.cloned.1.call-done = bf16[192,1024]{1,0:T(8,128)(2,1)} async-done(((bf16[1536,1024]{1,0:T(8,128)(2,1)}), bf16[192,1024]{1,0:T(8,128)(2,1)}) %reduce-scatter.25.cloned.1.call-update) | async-done | bytes 393232 | tf_op jit(solution)/shard_map/reduce_scatter | solution.py:135
  598.2 42.8 %reduce-scatter.27.cloned.1.call-done = bf16[192,1024]{1,0:T(8,128)(2,1)} async-done(((bf16[1536,1024]{1,0:T(8,128)(2,1)}), bf16[192,1024]{1,0:T(8,128)(2,1)}) %reduce-scatter.27.cloned.1.call-update) | async-done | bytes 393232 | tf_op jit(solution)/shard_map/reduce_scatter | solution.py:135
  642.9 32.7 %reduce-scatter.23.cloned.1.call-done = bf16[1,192,384]{2,1,0:T(8,128)(2,1)} async-done(((bf16[8,192,384]{2,1,0:T(8,128)(2,1)}), bf16[1,192,384]{2,1,0:T(8,128)(2,1)}) %reduce-scatter.23.cloned.1.call-update) | async-done | bytes 147472 | tf_op jit(solution)/shard_map/reduce_scatter | solution.py:128
  680.1 32.6 %reduce-scatter.21.cloned.1.call-done = bf16[192,768]{1,0:T(8,128)(2,1)} async-done(((bf16[1536,768]{1,0:T(8,128)(2,1)}), bf16[192,768]{1,0:T(8,128)(2,1)}) %reduce-scatter.21.cloned.1.call-update) | async-done | bytes 294928 | tf_op jit(solution)/shard_map/reduce_scatter | solution.py:135
  714.5 46.8 %reduce-scatter.19.cloned.1.call-done = bf16[256,1536]{1,0:T(8,128)(2,1)} async-done(((bf16[1024,1536]{1,0:T(8,128)(2,1)}), bf16[256,1536]{1,0:T(8,128)(2,1)}) %reduce-scatter.19.cloned.1.call-update) | async-done | bytes 786448 | tf_op jit(solution)/shard_map/reduce_scatter | solution.py:143
  764.9 43.3 %reduce-scatter.15.cloned.1.call-done = bf16[256,1536]{1,0:T(8,128)(2,1)} async-done(((bf16[1024,1536]{1,0:T(8,128)(2,1)}), bf16[256,1536]{1,0:T(8,128)(2,1)}) %reduce-scatter.15.cloned.1.call-update) | async-done | bytes 786448 | tf_op jit(solution)/shard_map/reduce_scatter | solution.py:143
  808.2 4.1 fusion.36
  812.3 96.4 %reduce-scatter.31.cloned.1.call-done = f32[48,2]{1,0:T(8,128)} async-done(((f32[1536,2]{1,0:T(8,128)}), f32[48,2]{1,0:T(8,128)}) %reduce-scatter.31.cloned.1.call-update) | async-done | bytes 400
  (283 shorter events, 130.7 us)
Async XLA Ops:
  7.2 128.7 %all-gather.18.cloned.1.call-start = ((), (), s32[]{:S(2)}) async-start(), calls=%async_computation.23 | async-start | bytes 1327104 | tf_op jit(solution)/shard_map/all_gather | solution.py:120
  7.2 1.7 collective-permute-start.7
  9.6 129.6 %all-gather.10.cloned.1.call-start = ((), (), s32[]{:S(2)}) async-start(), calls=%async_computation.10 | async-start | bytes 3932160 | tf_op jit(solution)/shard_map/all_gather | solution.py:140
  10.4 204.4 %reduce-scatter.13.cloned.1.call-start = ((), (), s32[]{:S(2)}) async-start(), calls=%async_computation.11 | async-start | bytes 3932160 | tf_op jit(solution)/shard_map/reduce_scatter | solution.py:143
  10.4 87.9 %collective-permute-start = (bf16[192,768]{1,0:T(8,128)(2,1)}, bf16[192,768]{1,0:T(8,128)(2,1)S(1)}, u32[]{:S(2)}, u32[]{:S(2)}) collective-permute-start(bf16[192,768]{1,0:T(8,128)(2,1)} %param.15), channel_id=1, source_target_pairs={{0,4},{4,8},{8,12},{12,16},{16,20},{20,24},{24,28},{28,0},{1,5},{5... | collective-permute-start | bytes 884744 | tf_op jit(solution)/shard_map/ppermute | solution.py:19
  17.4 90.6 %collective-permute-start.4 = (bf16[192,768]{1,0:T(8,128)(2,1)}, bf16[192,768]{1,0:T(8,128)(2,1)S(1)}, u32[]{:S(2)}, u32[]{:S(2)}) collective-permute-start(bf16[192,768]{1,0:T(8,128)(2,1)} %param.15), channel_id=1, source_target_pairs={{0,28},{4,0},{8,4},{12,8},{16,12},{20,16},{24,20},{28,24},{1,29},{... | collective-permute-start | bytes 884744 | tf_op jit(solution)/shard_map/ppermute | solution.py:21
  98.3 8.1 collective-permute-start.1
  106.5 8.9 collective-permute-start.2
  108.0 8.1 collective-permute-start.5
  115.4 8.6 collective-permute-start.3
  116.1 13.2 %collective-permute-start.6 = (bf16[192,768]{1,0:T(8,128)(2,1)S(1)}, bf16[192,768]{1,0:T(8,128)(2,1)S(1)}, u32[]{:S(2)}, u32[]{:S(2)}) collective-permute-start(bf16[192,768]{1,0:T(8,128)(2,1)S(1)} %collective-permute-done.5), channel_id=1, source_target_pairs={{0,28},{4,0},{8,4},{12,8},{16,12},{20,16},{24,20},{28,24},{1,29},{... | collective-permute-start | bytes 884744 | tf_op jit(solution)/shard_map/ppermute | solution.py:21
  147.5 365.1 %copy-start.11 = (bf16[1024,4,96]{0,2,1:T(8,128)(2,1)}, bf16[1024,4,96]{0,2,1:T(8,128)(2,1)S(1)}, u32[]{:S(2)}) copy-start(bf16[1024,4,96]{0,2,1:T(8,128)(2,1)S(1)} %get-tuple-element.33) | copy-start | bytes 2359300
  166.9 148.6 %all-gather.20.cloned.1.call-start = ((), (), s32[]{:S(2)}) async-start(), calls=%async_computation.24 | async-start | bytes 3538944 | tf_op jit(solution)/shard_map/all_gather | solution.py:120
  168.0 0.7 collective-permute-start.22
  169.4 152.6 %all-gather.14.cloned.1.call-start = ((), (), s32[]{:S(2)}) async-start(), calls=%async_computation.14 | async-start | bytes 3932160 | tf_op jit(solution)/shard_map/all_gather | solution.py:140
  170.0 197.5 %all-gather.12.cloned.1.call-start = ((), (), s32[]{:S(2)}) async-start(), calls=%async_computation.12 | async-start | bytes 3932160 | tf_op jit(solution)/shard_map/all_gather | solution.py:140
  219.2 221.1 %reduce-scatter.17.cloned.1.call-start = ((), (), s32[]{:S(2)}) async-start(), calls=%async_computation.15 | async-start | bytes 3932160 | tf_op jit(solution)/shard_map/reduce_scatter | solution.py:143
  219.2 9.2 collective-permute-start.15
  219.3 22.1 %collective-permute-start.8 = (bf16[192,1024]{1,0:T(8,128)(2,1)S(1)}, bf16[192,1024]{1,0:T(8,128)(2,1)S(1)}, u32[]{:S(2)}, u32[]{:S(2)}) collective-permute-start(bf16[192,1024]{1,0:T(8,128)(2,1)S(1)} %copy-done.28), channel_id=1, source_target_pairs={{0,4},{4,8},{8,12},{12,16},{16,20},{20,24},{24,28},{28,0},{1,5},{5... | collective-permute-start | bytes 1179656 | tf_op jit(solution)/shard_map/ppermute | solution.py:19
  228.4 29.9 %collective-permute-start.16 = (bf16[192,1024]{1,0:T(8,128)(2,1)S(1)}, bf16[192,1024]{1,0:T(8,128)(2,1)S(1)}, u32[]{:S(2)}, u32[]{:S(2)}) collective-permute-start(bf16[192,1024]{1,0:T(8,128)(2,1)S(1)} %collective-permute-done.15), channel_id=1, source_target_pairs={{0,4},{4,8},{8,12},{12,16},{16,20},{20,24},{24,28},{28,0},{1,5},{5... | collective-permute-start | bytes 1179656 | tf_op jit(solution)/shard_map/ppermute | solution.py:19
  228.4 29.9 %collective-permute-start.12 = (bf16[192,1024]{1,0:T(8,128)(2,1)S(1)}, bf16[192,1024]{1,0:T(8,128)(2,1)S(1)}, u32[]{:S(2)}, u32[]{:S(2)}) collective-permute-start(bf16[192,1024]{1,0:T(8,128)(2,1)S(1)} %copy-done.28), channel_id=1, source_target_pairs={{0,28},{4,0},{8,4},{12,8},{16,12},{20,16},{24,20},{28,24},{1,29},{... | collective-permute-start | bytes 1179656 | tf_op jit(solution)/shard_map/ppermute | solution.py:21
  231.9 34.7 %collective-permute-start.19 = (bf16[192,1024]{1,0:T(8,128)(2,1)S(1)}, bf16[192,1024]{1,0:T(8,128)(2,1)S(1)}, u32[]{:S(2)}, u32[]{:S(2)}) collective-permute-start(bf16[192,1024]{1,0:T(8,128)(2,1)S(1)} %copy-done.27), channel_id=1, source_target_pairs={{0,28},{4,0},{8,4},{12,8},{16,12},{20,16},{24,20},{28,24},{1,29},{... | collective-permute-start | bytes 1179656 | tf_op jit(solution)/shard_map/ppermute | solution.py:21
  241.4 31.8 %collective-permute-start.9 = (bf16[192,1024]{1,0:T(8,128)(2,1)S(1)}, bf16[192,1024]{1,0:T(8,128)(2,1)S(1)}, u32[]{:S(2)}, u32[]{:S(2)}) collective-permute-start(bf16[192,1024]{1,0:T(8,128)(2,1)S(1)} %collective-permute-done.8), channel_id=1, source_target_pairs={{0,4},{4,8},{8,12},{12,16},{16,20},{20,24},{24,28},{28,0},{1,5},{5... | collective-permute-start | bytes 1179656 | tf_op jit(solution)/shard_map/ppermute | solution.py:19
  258.2 24.0 %collective-permute-start.17 = (bf16[192,1024]{1,0:T(8,128)(2,1)S(1)}, bf16[192,1024]{1,0:T(8,128)(2,1)S(1)}, u32[]{:S(2)}, u32[]{:S(2)}) collective-permute-start(bf16[192,1024]{1,0:T(8,128)(2,1)S(1)} %collective-permute-done.16), channel_id=1, source_target_pairs={{0,4},{4,8},{8,12},{12,16},{16,20},{20,24},{24,28},{28,0},{1,5},{5... | collective-permute-start | bytes 1179656 | tf_op jit(solution)/shard_map/ppermute | solution.py:19
  258.3 24.1 %collective-permute-start.13 = (bf16[192,1024]{1,0:T(8,128)(2,1)S(1)}, bf16[192,1024]{1,0:T(8,128)(2,1)S(1)}, u32[]{:S(2)}, u32[]{:S(2)}) collective-permute-start(bf16[192,1024]{1,0:T(8,128)(2,1)S(1)} %collective-permute-done.12), channel_id=1, source_target_pairs={{0,28},{4,0},{8,4},{12,8},{16,12},{20,16},{24,20},{28,24},{1,29},{... | collective-permute-start | bytes 1179656 | tf_op jit(solution)/shard_map/ppermute | solution.py:21
  266.7 20.0 %collective-permute-start.20 = (bf16[192,1024]{1,0:T(8,128)(2,1)S(1)}, bf16[192,1024]{1,0:T(8,128)(2,1)S(1)}, u32[]{:S(2)}, u32[]{:S(2)}) collective-permute-start(bf16[192,1024]{1,0:T(8,128)(2,1)S(1)} %collective-permute-done.19), channel_id=1, source_target_pairs={{0,28},{4,0},{8,4},{12,8},{16,12},{20,16},{24,20},{28,24},{1,29},{... | collective-permute-start | bytes 1179656 | tf_op jit(solution)/shard_map/ppermute | solution.py:21
  273.2 17.5 %collective-permute-start.10 = (bf16[192,1024]{1,0:T(8,128)(2,1)S(1)}, bf16[192,1024]{1,0:T(8,128)(2,1)S(1)}, u32[]{:S(2)}, u32[]{:S(2)}) collective-permute-start(bf16[192,1024]{1,0:T(8,128)(2,1)S(1)} %collective-permute-done.9), channel_id=1, source_target_pairs={{0,4},{4,8},{8,12},{12,16},{16,20},{20,24},{24,28},{28,0},{1,5},{5... | collective-permute-start | bytes 1179656 | tf_op jit(solution)/shard_map/ppermute | solution.py:19
  282.2 16.9 %collective-permute-start.18 = (bf16[192,1024]{1,0:T(8,128)(2,1)S(1)}, bf16[192,1024]{1,0:T(8,128)(2,1)S(1)}, u32[]{:S(2)}, u32[]{:S(2)}) collective-permute-start(bf16[192,1024]{1,0:T(8,128)(2,1)S(1)} %collective-permute-done.17), channel_id=1, source_target_pairs={{0,4},{4,8},{8,12},{12,16},{16,20},{20,24},{24,28},{28,0},{1,5},{5... | collective-permute-start | bytes 1179656 | tf_op jit(solution)/shard_map/ppermute | solution.py:19
  282.4 30.7 %collective-permute-start.14 = (bf16[192,1024]{1,0:T(8,128)(2,1)S(1)}, bf16[192,1024]{1,0:T(8,128)(2,1)S(1)}, u32[]{:S(2)}, u32[]{:S(2)}) collective-permute-start(bf16[192,1024]{1,0:T(8,128)(2,1)S(1)} %collective-permute-done.13), channel_id=1, source_target_pairs={{0,28},{4,0},{8,4},{12,8},{16,12},{20,16},{24,20},{28,24},{1,29},{... | collective-permute-start | bytes 1179656 | tf_op jit(solution)/shard_map/ppermute | solution.py:21
  286.7 26.4 %collective-permute-start.21 = (bf16[192,1024]{1,0:T(8,128)(2,1)S(1)}, bf16[192,1024]{1,0:T(8,128)(2,1)S(1)}, u32[]{:S(2)}, u32[]{:S(2)}) collective-permute-start(bf16[192,1024]{1,0:T(8,128)(2,1)S(1)} %collective-permute-done.20), channel_id=1, source_target_pairs={{0,28},{4,0},{8,4},{12,8},{16,12},{20,16},{24,20},{28,24},{1,29},{... | collective-permute-start | bytes 1179656 | tf_op jit(solution)/shard_map/ppermute | solution.py:21
  290.6 16.9 %collective-permute-start.11 = (bf16[192,1024]{1,0:T(8,128)(2,1)S(1)}, bf16[192,1024]{1,0:T(8,128)(2,1)S(1)}, u32[]{:S(2)}, u32[]{:S(2)}) collective-permute-start(bf16[192,1024]{1,0:T(8,128)(2,1)S(1)} %collective-permute-done.10), channel_id=1, source_target_pairs={{0,4},{4,8},{8,12},{12,16},{16,20},{20,24},{24,28},{28,0},{1,5},{5... | collective-permute-start | bytes 1179656 | tf_op jit(solution)/shard_map/ppermute | solution.py:19
  396.1 93.5 %all-gather.16.cloned.1.call-start = ((), (), s32[]{:S(2)}) async-start(), calls=%async_computation.16 | async-start | bytes 3932160 | tf_op jit(solution)/shard_map/all_gather | solution.py:140
  445.5 105.7 %reduce-scatter.29.cloned.1.call-start = ((), (), s32[]{:S(2)}) async-start(), calls=%async_computation.22 | async-start | bytes 3538944 | tf_op jit(solution)/shard_map/reduce_scatter | solution.py:128
  463.5 132.7 %reduce-scatter.25.cloned.1.call-start = ((), (), s32[]{:S(2)}) async-start(), calls=%async_computation.20 | async-start | bytes 3538944 | tf_op jit(solution)/shard_map/reduce_scatter | solution.py:135
  471.2 169.7 %reduce-scatter.27.cloned.1.call-start = ((), (), s32[]{:S(2)}) async-start(), calls=%async_computation.21 | async-start | bytes 3538944 | tf_op jit(solution)/shard_map/reduce_scatter | solution.py:135
  479.2 196.4 %reduce-scatter.23.cloned.1.call-start = ((), (), s32[]{:S(2)}) async-start(), calls=%async_computation.19 | async-start | bytes 1327104 | tf_op jit(solution)/shard_map/reduce_scatter | solution.py:128
  517.4 195.3 %reduce-scatter.21.cloned.1.call-start = ((), (), s32[]{:S(2)}) async-start(), calls=%async_computation.18 | async-start | bytes 2654208 | tf_op jit(solution)/shard_map/reduce_scatter | solution.py:135
  537.6 223.7 %reduce-scatter.19.cloned.1.call-start = ((), (), s32[]{:S(2)}) async-start(), calls=%async_computation.17 | async-start | bytes 3932160 | tf_op jit(solution)/shard_map/reduce_scatter | solution.py:143
  543.5 264.7 %reduce-scatter.15.cloned.1.call-start = ((), (), s32[]{:S(2)}) async-start(), calls=%async_computation.13 | async-start | bytes 3932160 | tf_op jit(solution)/shard_map/reduce_scatter | solution.py:143
  551.2 357.5 %reduce-scatter.31.cloned.1.call-start = ((), (), s32[]{:S(2)}) async-start(), calls=%async_computation.25 | async-start | bytes 811008
  551.2 127.1 %collective-permute-start.24 = (bf16[512,384]{1,0:T(8,128)(2,1)}, bf16[512,384]{1,0:T(8,128)(2,1)S(1)}, u32[]{:S(2)}, u32[]{:S(2)}) collective-permute-start(bf16[512,384]{1,0:T(8,128)(2,1)} %bitcast.252), channel_id=1, source_target_pairs={{0,0},{4,1},{8,2},{12,3},{16,4},{20,5},{24,6},{28,7},{1,8},{5,9},{... | collective-permute-start | bytes 1179656 | tf_op jit(solution)/shard_map/ppermute | solution.py:129
  642.9 165.2 %copy-start.4 = (bf16[256,1536]{1,0:T(8,128)(2,1)S(1)}, bf16[256,1536]{1,0:T(8,128)(2,1)}, u32[]{:S(2)}) copy-start(bf16[256,1536]{1,0:T(8,128)(2,1)} %param.13) | copy-start | bytes 2359300
  642.9 165.2 %copy-start.5 = (bf16[256,1536]{1,0:T(8,128)(2,1)S(1)}, bf16[256,1536]{1,0:T(8,128)(2,1)}, u32[]{:S(2)}) copy-start(bf16[256,1536]{1,0:T(8,128)(2,1)} %reduce-scatter.17.cloned.1.call-done) | copy-start | bytes 2359300
  675.6 3.8 collective-permute-start.23
  679.3 128.8 %copy-start.37 = (f32[256]{0:T(256)S(1)}, f32[256]{0:T(256)}, u32[]{:S(2)}) copy-start(f32[256]{0:T(256)} %get-tuple-element.42) | copy-start | bytes 3076
  679.3 128.9 %copy-start.39 = (f32[256]{0:T(256)S(1)}, f32[256]{0:T(256)}, u32[]{:S(2)}) copy-start(f32[256]{0:T(256)} %get-tuple-element.43) | copy-start | bytes 3076
  679.3 128.9 %copy-start.41 = (f32[256]{0:T(256)S(1)}, f32[256]{0:T(256)}, u32[]{:S(2)}) copy-start(f32[256]{0:T(256)} %copy-done.40) | copy-start | bytes 3076
  679.3 128.9 %copy-start.48 = (f32[256]{0:T(256)S(1)}, f32[256]{0:T(256)}, u32[]{:S(2)}) copy-start(f32[256]{0:T(256)} %get-tuple-element.41) | copy-start | bytes 3076
  (52 other events, 848.2 us)
Sparse Core Ops, SparseCore 0:
  10.2 34.4 all-gather.17
  46.6 43.4 all-gather.9
  167.0 47.6 reduce-scatter.12
  216.8 56.2 all-gather.19
  274.8 46.3 all-gather.13
  323.5 43.9 all-gather.11
  396.3 43.9 reduce-scatter.16
  445.6 43.9 all-gather.15
  491.9 40.3 reduce-scatter.28
  534.4 61.7 reduce-scatter.24
  598.5 42.3 reduce-scatter.26
  643.7 31.8 reduce-scatter.22
  677.9 34.7 reduce-scatter.20
  715.6 45.7 reduce-scatter.18
  764.2 43.9 reduce-scatter.14
  813.1 95.4 reduce-scatter.30
